TPU v7x, 128 devices: a whole 4x4x4 slice. The times are simulated.
128 devices in a mesh: ctx: 8 (over x, z_lo), fsdp: 16 (over z_hi, y, core).
Axes of the slice: x: 4, y: 4, z: 4 (z_hi: 2, z_lo: 2; z = z_hi * 2 + z_lo), core: 2. Of those that a mesh axis runs over, the one named last changes fastest.
Arguments:
- inputs: bfloat16 [16, 1024, 1152], P('fsdp', 'ctx'), may hold values from -6 to 6
- out_grad: bfloat16 [16, 1024, 1152], P('fsdp', 'ctx'), may hold values from -6 to 6
- positions: int32 [16, 1024], P('fsdp', 'ctx'), may hold values from 0 to 1023, as said below
- block_order: int32 [8, 2], replicated, may hold values from 0 to 15, as said below
- w_query: bfloat16 [1152, 1024], P('fsdp'), may hold values from -0.1875 to 0.1875
- w_key: bfloat16 [1152, 256], P('fsdp'), may hold values from -0.1875 to 0.1875
- w_value: bfloat16 [1152, 256], P('fsdp'), may hold values from -0.1875 to 0.1875
- w_output: bfloat16 [1024, 1152], P(None, 'fsdp'), may hold values from -0.1875 to 0.1875
- w_gate: bfloat16 [6912, 1152], P('fsdp'), may hold values from -0.1875 to 0.1875
- w_up: bfloat16 [6912, 1152], P('fsdp'), may hold values from -0.1875 to 0.1875
- w_down: bfloat16 [6912, 1152], P('fsdp'), may hold values from -0.078125 to 0.078125
- gain_in: bfloat16 [1152], P('fsdp'), may hold values from 0.099609375 to 1.8984375
- gain_query: bfloat16 [256], P('fsdp'), may hold values from 0.099609375 to 1.8984375
- gain_key: bfloat16 [256], P('fsdp'), may hold values from 0.099609375 to 1.8984375
- gain_attn: bfloat16 [1152], P('fsdp'), may hold values from 0.099609375 to 1.8984375
- gain_pre: bfloat16 [1152], P('fsdp'), may hold values from 0.099609375 to 1.8984375
- gain_post: bfloat16 [1152], P('fsdp'), may hold values from 0.099609375 to 1.8984375
Outputs:
- outputs: bfloat16 [16, 1024, 1152], P('fsdp', 'ctx')
- in_grad: bfloat16 [16, 1024, 1152], P('fsdp', 'ctx')
- grad_w_query: float32 [1152, 1024], P('fsdp')
- grad_w_key: float32 [1152, 256], P('fsdp')
- grad_w_value: float32 [1152, 256], P('fsdp')
- grad_w_output: float32 [1024, 1152], P(None, 'fsdp')
- grad_w_gate: float32 [6912, 1152], P('fsdp')
- grad_w_up: float32 [6912, 1152], P('fsdp')
- grad_w_down: float32 [6912, 1152], P('fsdp')
- grad_gain_in: float32 [1152], P('fsdp')
- grad_gain_query: float32 [256], P('fsdp')
- grad_gain_key: float32 [256], P('fsdp')
- grad_gain_attn: float32 [1152], P('fsdp')
- grad_gain_pre: float32 [1152], P('fsdp')
- grad_gain_post: float32 [1152], P('fsdp')
Inputs may be any that keep to these rules, and one draw needn't show every extreme that they name: `block_order`: row c names the two blocks of 64 tokens in device c's rows, in order; every block appears once, and a row holds blocks k and m with k + m one less than the number of blocks. `positions`: each row's offset from the start of its document in the sequence; documents begin at the sequence's first token and at random places; sequence 0 is one document.
All inputs are finite; a program needn't handle non-finite values.
Results may differ from a plain program's by a relative error of at most 0.03.
Values may be sent and summed in bfloat16 or wider, within the bound.
No kernel may reach another device: no remote copies, remote signals or barrier semaphores. Data moves between devices by JAX's collectives and lax.ppermute only.
A program may use at most 128 MiB of HBM per device.

v0:
```python
import jax
import jax.numpy as jnp
from jax import lax
from jax.sharding import PartitionSpec as P

H = 4
HD = 256
EPS = 1e-06
ROPE_BASE = 1000000.0
GELU_C = 0.7978845608028654
GELU_A = 0.044715


def norm_forward(values, gain):
    inverse = lax.rsqrt(jnp.mean(values * values, axis=-1, keepdims=True) + EPS)
    unit = values * inverse
    return (unit * gain, unit, inverse)


def norm_backward(upstream, unit, inverse, gain):
    scaled = upstream * gain
    inner = jnp.mean(scaled * unit, axis=-1, keepdims=True)
    leading = tuple(range(upstream.ndim - 1))
    return (inverse * (scaled - unit * inner), jnp.sum(upstream * unit, axis=leading))


def gelu_pair(gate):
    inner = GELU_C * (gate + GELU_A * gate * gate * gate)
    tangent = jnp.tanh(inner)
    value = 0.5 * gate * (1.0 + tangent)
    slope = 0.5 * (1.0 + tangent) + 0.5 * gate * (1.0 - tangent * tangent) * GELU_C * (
        1.0 + 3.0 * GELU_A * gate * gate
    )
    return (value, slope)


def rope_tables(positions, width):
    half = width // 2
    freqs = ROPE_BASE ** (-2.0 * jnp.arange(half, dtype=jnp.float32) / width)
    angles = positions.astype(jnp.float32)[:, None] * freqs[None, :]
    return (jnp.cos(angles), jnp.sin(angles))


def rotate(values, cosine, sine):
    half = values.shape[-1] // 2
    first = values[..., :half]
    second = values[..., half:]
    return jnp.concatenate(
        [first * cosine - second * sine, second * cosine + first * sine], axis=-1
    )


def rotate_back(values, cosine, sine):
    half = values.shape[-1] // 2
    first = values[..., :half]
    second = values[..., half:]
    return jnp.concatenate(
        [first * cosine + second * sine, second * cosine - first * sine], axis=-1
    )


def sequence_rows(order_flat, first_row, count, block):
    rows = first_row + jnp.arange(count, dtype=jnp.int32)
    slots = rows // block
    table = jnp.arange(order_flat.shape[0], dtype=jnp.int32)
    picked = jnp.sum(jnp.where(slots[:, None] == table[None, :], order_flat[None, :], 0), axis=1)
    return picked * block + rows % block


def body(
    inputs,
    out_grad,
    positions,
    block_order,
    w_query,
    w_key,
    w_value,
    w_output,
    w_gate,
    w_up,
    w_down,
    gain_in,
    gain_query,
    gain_key,
    gain_attn,
    gain_pre,
    gain_post,
):
    f32 = jnp.float32
    low = jnp.bfloat16
    tokens = inputs[0]
    local = tokens.shape[0]
    parts = lax.axis_size("ctx")
    total = local * parts
    block = local // 2
    gathered = (
        lax.all_gather(w_query, "fsdp", axis=0, tiled=True),
        lax.all_gather(w_key, "fsdp", axis=0, tiled=True),
        lax.all_gather(w_value, "fsdp", axis=0, tiled=True),
        lax.all_gather(w_output, "fsdp", axis=1, tiled=True),
        lax.all_gather(gain_in, "fsdp", axis=0, tiled=True),
        lax.all_gather(gain_query, "fsdp", axis=0, tiled=True),
        lax.all_gather(gain_key, "fsdp", axis=0, tiled=True),
        lax.all_gather(gain_attn, "fsdp", axis=0, tiled=True),
        lax.all_gather(gain_pre, "fsdp", axis=0, tiled=True),
        lax.all_gather(gain_post, "fsdp", axis=0, tiled=True),
    )
    full_query, full_key, full_value, full_output = (
        gathered[0],
        gathered[1],
        gathered[2],
        gathered[3],
    )
    norm_in, norm_query, norm_key, norm_attn, norm_pre, norm_post = [
        g.astype(f32) for g in gathered[4:]
    ]
    ctx_index = lax.axis_index("ctx")
    order_flat = block_order.reshape(-1)
    my_seq = sequence_rows(order_flat, ctx_index * local, local, block)
    all_seq = sequence_rows(order_flat, 0, total, block)
    flat_in = tokens.astype(f32)
    normed_full, unit_in, inv_in = norm_forward(flat_in, norm_in)
    normed_in = normed_full.astype(low)
    queries = jnp.dot(normed_in, full_query, preferred_element_type=f32).reshape(local, H, HD)
    keys_raw = jnp.dot(normed_in, full_key, preferred_element_type=f32)
    values = jnp.dot(normed_in, full_value, preferred_element_type=f32).astype(low)
    query_normed, query_unit, query_inv = norm_forward(queries, norm_query)
    key_normed, key_unit, key_inv = norm_forward(keys_raw, norm_key)
    cosine, sine = rope_tables(positions[0], HD)
    scale = HD ** (-0.5)
    query_rot = (rotate(query_normed, cosine[:, None, :], sine[:, None, :]) * scale).astype(low)
    key_rot = rotate(key_normed, cosine, sine).astype(low)
    key_all, value_all = (
        lax.all_gather(key_rot, "ctx", axis=0, tiled=True),
        lax.all_gather(values, "ctx", axis=0, tiled=True),
    )
    scores = jnp.einsum("qhd,kd->hqk", query_rot, key_all, preferred_element_type=f32)
    allowed = my_seq[:, None] >= all_seq[None, :]
    scores = jnp.where(allowed[None], scores, -jnp.inf)
    highest = jnp.max(scores, axis=-1, keepdims=True)
    log_total = highest + jnp.log(jnp.sum(jnp.exp(scores - highest), axis=-1, keepdims=True))
    probs_full = jnp.exp(scores - log_total)
    probs = probs_full.astype(low)
    attended = (
        jnp.einsum("hqk,kd->qhd", probs, value_all, preferred_element_type=f32)
        .reshape(local, H * HD)
        .astype(low)
    )
    branch_attn = jnp.dot(attended, full_output, preferred_element_type=f32)
    attn_normed, attn_unit, attn_inv = norm_forward(branch_attn, norm_attn)
    residual = flat_in + attn_normed
    pre_full, pre_unit, pre_inv = norm_forward(residual, norm_pre)
    normed_pre = pre_full.astype(low)
    rows_all = lax.all_gather(normed_pre, "fsdp", axis=0, tiled=True)
    gate = jnp.einsum("td,fd->tf", rows_all, w_gate, preferred_element_type=f32)
    upper = jnp.einsum("td,fd->tf", rows_all, w_up, preferred_element_type=f32)
    gelu_value, gelu_slope = gelu_pair(gate)
    hidden = (gelu_value * upper).astype(low)
    branch_ffn = lax.psum_scatter(
        jnp.dot(hidden, w_down, preferred_element_type=f32).astype(jnp.bfloat16),
        "fsdp",
        scatter_dimension=0,
        tiled=True,
    ).astype(jnp.float32)
    post_normed, post_unit, post_inv = norm_forward(branch_ffn, norm_post)
    outputs = (residual + post_normed).astype(low)
    grad_out = out_grad[0].astype(f32)
    grad_ffn_full, grad_gain_post = norm_backward(grad_out, post_unit, post_inv, norm_post)
    grad_ffn = grad_ffn_full.astype(low)
    grad_all = lax.all_gather(grad_ffn, "fsdp", axis=0, tiled=True)
    grad_hidden = jnp.einsum("td,fd->tf", grad_all, w_down, preferred_element_type=f32)
    grad_gate = (grad_hidden * upper * gelu_slope).astype(low)
    grad_up = (grad_hidden * gelu_value).astype(low)
    shard_gate = jnp.einsum("tf,td->fd", grad_gate, rows_all, preferred_element_type=f32)
    shard_up = jnp.einsum("tf,td->fd", grad_up, rows_all, preferred_element_type=f32)
    shard_down = jnp.einsum("tf,td->fd", hidden, grad_all, preferred_element_type=f32)
    grad_pre = lax.psum_scatter(
        (
            jnp.dot(grad_gate, w_gate, preferred_element_type=f32)
            + jnp.dot(grad_up, w_up, preferred_element_type=f32)
        ).astype(jnp.bfloat16),
        "fsdp",
        scatter_dimension=0,
        tiled=True,
    ).astype(jnp.float32)
    grad_from_pre, grad_gain_pre = norm_backward(grad_pre, pre_unit, pre_inv, norm_pre)
    grad_residual = grad_out + grad_from_pre
    grad_branch_full, grad_gain_attn = norm_backward(grad_residual, attn_unit, attn_inv, norm_attn)
    grad_branch = grad_branch_full.astype(low)
    term_output = jnp.einsum("tc,td->cd", attended, grad_branch, preferred_element_type=f32)
    grad_attended = jnp.einsum(
        "td,cd->tc", grad_branch, full_output, preferred_element_type=f32
    ).astype(low)
    grad_heads = grad_attended.reshape(local, H, HD)
    attended_heads = attended.reshape(local, H, HD)
    delta = jnp.transpose(jnp.sum(grad_heads.astype(f32) * attended_heads.astype(f32), axis=-1))[
        :, :, None
    ]
    grad_probs = jnp.einsum("qhd,kd->hqk", grad_heads, value_all, preferred_element_type=f32)
    grad_scores = (probs_full * (grad_probs - delta)).astype(low)
    value_term = jnp.einsum("hqk,qhd->kd", probs, grad_heads, preferred_element_type=f32)
    key_term = jnp.einsum("hqk,qhd->kd", grad_scores, query_rot, preferred_element_type=f32)
    key_value_terms = jnp.concatenate([key_term, value_term], axis=1)
    grad_query_rot = jnp.einsum("hqk,kd->qhd", grad_scores, key_all, preferred_element_type=f32)
    summed_kv = lax.psum_scatter(
        key_value_terms.astype(jnp.bfloat16), "ctx", scatter_dimension=0, tiled=True
    ).astype(jnp.float32)
    grad_key_rot = summed_kv[:, :HD]
    grad_values = summed_kv[:, HD:].astype(low)
    grad_q_normed = rotate_back(grad_query_rot * scale, cosine[:, None, :], sine[:, None, :])
    grad_q_full, grad_gain_query = norm_backward(grad_q_normed, query_unit, query_inv, norm_query)
    grad_k_normed = rotate_back(grad_key_rot, cosine, sine)
    grad_k_full, grad_gain_key = norm_backward(grad_k_normed, key_unit, key_inv, norm_key)
    grad_q_in = grad_q_full.reshape(local, H * HD).astype(low)
    grad_k_in = grad_k_full.astype(low)
    term_query = jnp.einsum("td,tc->dc", normed_in, grad_q_in, preferred_element_type=f32)
    term_key = jnp.einsum("td,tc->dc", normed_in, grad_k_in, preferred_element_type=f32)
    term_value = jnp.einsum("td,tc->dc", normed_in, grad_values, preferred_element_type=f32)
    grad_normed = (
        jnp.einsum("tc,dc->td", grad_q_in, full_query, preferred_element_type=f32)
        + jnp.einsum("tc,dc->td", grad_k_in, full_key, preferred_element_type=f32)
        + jnp.einsum("tc,dc->td", grad_values, full_value, preferred_element_type=f32)
    )
    grad_from_in, grad_gain_in = norm_backward(grad_normed, unit_in, inv_in, norm_in)
    in_grad = (grad_residual + grad_from_in).astype(low)
    shards = (
        lax.psum_scatter(
            term_query.astype(jnp.bfloat16), "fsdp", scatter_dimension=0, tiled=True
        ).astype(jnp.float32),
        lax.psum_scatter(
            term_key.astype(jnp.bfloat16), "fsdp", scatter_dimension=0, tiled=True
        ).astype(jnp.float32),
        lax.psum_scatter(
            term_value.astype(jnp.bfloat16), "fsdp", scatter_dimension=0, tiled=True
        ).astype(jnp.float32),
        lax.psum_scatter(
            term_output.astype(jnp.bfloat16), "fsdp", scatter_dimension=1, tiled=True
        ).astype(jnp.float32),
        lax.psum_scatter(
            grad_gain_in.astype(jnp.bfloat16), "fsdp", scatter_dimension=0, tiled=True
        ).astype(jnp.float32),
        lax.psum_scatter(
            grad_gain_query.astype(jnp.bfloat16), "fsdp", scatter_dimension=0, tiled=True
        ).astype(jnp.float32),
        lax.psum_scatter(
            grad_gain_key.astype(jnp.bfloat16), "fsdp", scatter_dimension=0, tiled=True
        ).astype(jnp.float32),
        lax.psum_scatter(
            grad_gain_attn.astype(jnp.bfloat16), "fsdp", scatter_dimension=0, tiled=True
        ).astype(jnp.float32),
        lax.psum_scatter(
            grad_gain_pre.astype(jnp.bfloat16), "fsdp", scatter_dimension=0, tiled=True
        ).astype(jnp.float32),
        lax.psum_scatter(
            grad_gain_post.astype(jnp.bfloat16), "fsdp", scatter_dimension=0, tiled=True
        ).astype(jnp.float32),
    )
    totals = (
        lax.psum(shards[0].astype(jnp.bfloat16), "ctx").astype(jnp.float32),
        lax.psum(shards[1].astype(jnp.bfloat16), "ctx").astype(jnp.float32),
        lax.psum(shards[2].astype(jnp.bfloat16), "ctx").astype(jnp.float32),
        lax.psum(shards[3].astype(jnp.bfloat16), "ctx").astype(jnp.float32),
        lax.psum(shard_gate.astype(jnp.bfloat16), "ctx").astype(jnp.float32),
        lax.psum(shard_up.astype(jnp.bfloat16), "ctx").astype(jnp.float32),
        lax.psum(shard_down.astype(jnp.bfloat16), "ctx").astype(jnp.float32),
        lax.psum(shards[4].astype(jnp.bfloat16), "ctx").astype(jnp.float32),
        lax.psum(shards[5].astype(jnp.bfloat16), "ctx").astype(jnp.float32),
        lax.psum(shards[6].astype(jnp.bfloat16), "ctx").astype(jnp.float32),
        lax.psum(shards[7].astype(jnp.bfloat16), "ctx").astype(jnp.float32),
        lax.psum(shards[8].astype(jnp.bfloat16), "ctx").astype(jnp.float32),
        lax.psum(shards[9].astype(jnp.bfloat16), "ctx").astype(jnp.float32),
    )
    return (
        outputs[None],
        in_grad[None],
        totals[0],
        totals[1],
        totals[2],
        totals[3],
        totals[4],
        totals[5],
        totals[6],
        totals[7],
        totals[8],
        totals[9],
        totals[10],
        totals[11],
        totals[12],
    )


def solution(mesh):
    placed = (
        P("fsdp", "ctx", None),
        P("fsdp", "ctx", None),
        P("fsdp", "ctx"),
        P(),
        P("fsdp", None),
        P("fsdp", None),
        P("fsdp", None),
        P(None, "fsdp"),
        P("fsdp", None),
        P("fsdp", None),
        P("fsdp", None),
        P("fsdp"),
        P("fsdp"),
        P("fsdp"),
        P("fsdp"),
        P("fsdp"),
        P("fsdp"),
    )
    return jax.shard_map(
        body,
        mesh=mesh,
        in_specs=placed,
        out_specs=(
            P("fsdp", "ctx", None),
            P("fsdp", "ctx", None),
            P("fsdp", None),
            P("fsdp", None),
            P("fsdp", None),
            P(None, "fsdp"),
            P("fsdp", None),
            P("fsdp", None),
            P("fsdp", None),
            P("fsdp"),
            P("fsdp"),
            P("fsdp"),
            P("fsdp"),
            P("fsdp"),
            P("fsdp"),
        ),
        check_vma=False,
    )
```

profile of v0, /device:TPU:8, one launch (start us, length us, event | category | flops | bytes accessed | tf_op | source)
XLA Modules:
  0.0 1100.2 jit_solution(11387176566763124986)
XLA Ops:
  8.8 1.3 fusion.101
  18.5 65.3 %all-reduce.13 = (bf16[1152]{0:T(1024)(128)(2,1)S(1)}, bf16[256]{0:T(256)(128)(2,1)S(1)}, bf16[256]{0:T(256)(128)(2,1)S(1)}, bf16[1152]{0:T(1024)(128)(2,1)S(1)}...) all-reduce(bf16[1152]{0:T(1024)(128)(2,1)S(1)} %dynamic-update-slic, ...), channel_id=1, replica_groups=mesh['ctx'=8,'fsdp'=16] {'fsdp'}, use_global_device_ids=true, to_apply=%add | all-reduce | flops 5120 | bytes 20480
  83.8 26.9 %all_gather.45 = bf16[1152,256]{1,0:T(8,128)(2,1)S(1)} all-gather(bf16[72,256]{1,0:T(8,128)(2,1)} %param.22), channel_id=1, replica_groups=mesh['ctx'=8,'fsdp'=16] {'fsdp'}, dimensions={0}, use_global_device_ids=true | all-gather | bytes 626688 | tf_op jit(solution)/shard_map/all_gather | solution.py:98
  110.8 1.5 multiply_reduce_fusion.10
  113.2 29.1 %all_gather.47 = bf16[1024,256]{1,0:T(8,128)(2,1)S(1)} all-gather(bf16[128,256]{1,0:T(8,128)(2,1)S(1)} %pad_maximum_fusion.3), channel_id=1, replica_groups=mesh['ctx'=8,'fsdp'=16] {'ctx'}, dimensions={0}, use_global_device_ids=true | all-gather | bytes 589824 | tf_op jit(solution)/shard_map/all_gather | solution.py:134
  142.3 21.9 %all_gather.43 = bf16[1152,256]{1,0:T(8,128)(2,1)S(1)} all-gather(bf16[72,256]{1,0:T(8,128)(2,1)S(1)} %copy-done.39), channel_id=1, replica_groups=mesh['ctx'=8,'fsdp'=16] {'fsdp'}, dimensions={0}, use_global_device_ids=true | all-gather | bytes 626688 | tf_op jit(solution)/shard_map/all_gather | solution.py:99
  165.3 29.2 %all_gather.44 = bf16[1024,256]{1,0:T(8,128)(2,1)S(1)} all-gather(bf16[128,256]{1,0:T(8,128)(2,1)S(1)} %convolution_convert_fusion.10), channel_id=1, replica_groups=mesh['ctx'=8,'fsdp'=16] {'ctx'}, dimensions={0}, use_global_device_ids=true | all-gather | bytes 589824 | tf_op jit(solution)/shard_map/all_gather | solution.py:135
  194.6 4.5 copy.77
  199.0 2.6 multiply_reduce_fusion.7
  205.1 2.7 multiply_reduce_fusion.3
  209.2 55.1 %all-gather.9.cloned.1.call-done = bf16[2048,1152]{1,0:T(8,128)(2,1)} async-done(((bf16[128,1152]{1,0:T(8,128)(2,1)}), bf16[2048,1152]{1,0:T(8,128)(2,1)}) %all-gather.9.cloned.1.call-update) | async-done | bytes 4718608 | tf_op jit(solution)/shard_map/all_gather | solution.py:154
  264.3 5.2 fusion.102
  269.6 4.6 multiply_convert_fusion.1
  275.5 4.6 convolution_convert_fusion
  280.2 81.5 %reduce-scatter.8.cloned.1.call-done = bf16[128,1152]{1,0:T(8,128)(2,1)} async-done(((bf16[2048,1152]{1,0:T(8,128)(2,1)}), bf16[128,1152]{1,0:T(8,128)(2,1)}) %reduce-scatter.8.cloned.1.call-update) | async-done | bytes 294928 | tf_op jit(solution)/shard_map/reduce_scatter | solution.py:159
  362.8 1.3 fusion.46
  364.1 1.9 fusion.28
  366.3 56.5 %all-gather.11.cloned.1.call-done = bf16[2048,1152]{1,0:T(8,128)(2,1)} async-done(((bf16[128,1152]{1,0:T(8,128)(2,1)}), bf16[2048,1152]{1,0:T(8,128)(2,1)}) %all-gather.11.cloned.1.call-update) | async-done | bytes 4718608 | tf_op jit(solution)/shard_map/all_gather | solution.py:170
  422.8 8.5 multiply_convert_fusion
  431.4 3.0 fusion.103
  434.4 4.6 add_convert_fusion
  439.1 81.6 %reduce-scatter.10.cloned.1.call-done = bf16[128,1152]{1,0:T(8,128)(2,1)} async-done(((bf16[2048,1152]{1,0:T(8,128)(2,1)}), bf16[128,1152]{1,0:T(8,128)(2,1)}) %reduce-scatter.10.cloned.1.call-update) | async-done | bytes 294928 | tf_op jit(solution)/shard_map/reduce_scatter | solution.py:177
  520.7 1.3 fusion.35
  522.0 2.3 multiply_reduce_fusion
  524.5 1.2 convolution_convert_fusion.8
  525.8 1.8 copy.80
  528.8 1.5 fusion.12
  533.6 38.6 %reduce-scatter.12.cloned.1.call-done = bf16[128,512]{1,0:T(8,128)(2,1)} async-done(((bf16[1024,512]{1,0:T(8,128)(2,1)}), bf16[128,512]{1,0:T(8,128)(2,1)}) %reduce-scatter.12.cloned.1.call-update) | async-done | bytes 131088 | tf_op jit(solution)/shard_map/reduce_scatter | solution.py:205
  572.3 2.1 convolution_convert_fusion.6
  576.0 1.2 convolution_convert_fusion.7
  577.3 2.2 convolution_convert_fusion.1
  581.4 2.4 convolution_convert_fusion.2
  585.2 6.5 convolution_convert_fusion.3
  591.7 3.4 convolution_convert_fusion.4
  597.0 60.0 %all-reduce.12 = (bf16[1152]{0:T(1024)(128)(2,1)S(1)}, bf16[256]{0:T(256)(128)(2,1)S(1)}, bf16[256]{0:T(256)(128)(2,1)S(1)}, bf16[1152]{0:T(1024)(128)(2,1)S(1)}...) all-reduce(bf16[1152]{0:T(1024)(128)(2,1)S(1)} %get-tuple-element.2, ...), channel_id=9, replica_groups=mesh['ctx'=8,'fsdp'=16] {'fsdp'}, use_global_device_ids=true, to_apply=%region_32.33.clone | all-reduce | flops 5120 | bytes 20480
  660.5 45.4 %reduce-scatter.16.cloned.1.call-done = bf16[72,256]{1,0:T(8,128)(2,1)} async-done(((bf16[1152,256]{1,0:T(8,128)(2,1)}), bf16[72,256]{1,0:T(8,128)(2,1)}) %reduce-scatter.16.cloned.1.call-update) | async-done | bytes 36880 | tf_op jit(solution)/shard_map/reduce_scatter | solution.py:230
  706.0 6.3 convolution_convert_fusion.5
  712.3 68.7 %reduce-scatter.20.cloned.1.call-done = bf16[1024,72]{0,1:T(8,128)(2,1)} async-done(((bf16[1024,1152]{0,1:T(8,128)(2,1)}), bf16[1024,72]{0,1:T(8,128)(2,1)}) %reduce-scatter.20.cloned.1.call-update) | async-done | bytes 147472 | tf_op jit(solution)/shard_map/reduce_scatter | solution.py:236
  781.0 75.3 %reduce-scatter.14.cloned.1.call-done = bf16[72,1024]{1,0:T(8,128)(2,1)} async-done(((bf16[1152,1024]{1,0:T(8,128)(2,1)}), bf16[72,1024]{1,0:T(8,128)(2,1)}) %reduce-scatter.14.cloned.1.call-update) | async-done | bytes 147472 | tf_op jit(solution)/shard_map/reduce_scatter | solution.py:227
  857.3 71.0 %all-reduce.19.cloned.1.call-done = (bf16[72,256]{1,0:T(8,128)(2,1)}, bf16[72,256]{1,0:T(8,128)(2,1)}, bf16[72]{0:T(256)(128)(2,1)}, bf16[16]{0:T(256)(128)(2,1)...) async-done(((bf16[72,256]{1,0:T(8,128)(2,1)}, bf16[72,256]{1,0:T(8,128)(2,1)}, bf16[72]{0:T(256)(128)(2,1)}, ...) | async-done | bytes 74384 | tf_op jit(solution)/shard_map/psum | solution.py:260
  935.2 1.4 convert_element_type.281
  936.6 1.4 convert_element_type.283
  938.0 146.8 %all-reduce.21.cloned.1.call-done = (bf16[72,1024]{1,0:T(8,128)(2,1)}, bf16[1024,72]{0,1:T(8,128)(2,1)}, bf16[432,1152]{1,0:T(8,128)(2,1)}, bf16[432,1152]{1,0:T(8,128)(2,1)}, bf16[432,1152]{1,0:T(8,128)(2,1)}) async-done(((bf16[72,1024]{1,0:T(8,128)(2,1)}, bf16[1024,72]{0,1:T(8,128)(2,1)}, bf16[432,1152]{1,0:T(8,128)(2,1)}, bf16[432,1152]{1,0:T(8,128)(2,1)}, bf16[432,1152]{1,0:T(8,128)(2,1)}), ...) | async-done | bytes 3280912 | tf_op jit(solution)/shard_map/psum | solution.py:259
  1084.8 1.7 convert_element_type.279
  1086.5 1.6 convert_element_type.285
  1088.1 2.7 convert_element_type.287
  1090.8 1.4 convert_element_type.289
  1092.2 1.4 convert_element_type.291
  (227 shorter events, 39.3 us)
Async XLA Ops:
  7.2 268.3 %copy-start = (bf16[432,1152]{1,0:T(8,128)(2,1)S(1)}, bf16[432,1152]{1,0:T(8,128)(2,1)}, u32[]{:S(2)}) copy-start(bf16[432,1152]{1,0:T(8,128)(2,1)} %param.27) | copy-start | bytes 2985988
  7.2 157.8 %copy-start.2 = (bf16[1,128,1152]{2,1,0:T(8,128)(2,1)S(1)}, bf16[1,128,1152]{2,1,0:T(8,128)(2,1)}, u32[]{:S(2)}) copy-start(bf16[1,128,1152]{2,1,0:T(8,128)(2,1)} %param.17) | copy-start | bytes 884740
  7.2 105.3 %copy-start.48 = (s32[1,128]{1,0:T(1,128)S(1)}, s32[1,128]{1,0:T(1,128)}, u32[]{:S(2)}) copy-start(s32[1,128]{1,0:T(1,128)} %param.19) | copy-start | bytes 1540
  7.2 135.1 %copy-start.39 = (bf16[72,256]{1,0:T(8,128)(2,1)S(1)}, bf16[72,256]{1,0:T(8,128)(2,1)}, u32[]{:S(2)}) copy-start(bf16[72,256]{1,0:T(8,128)(2,1)} %param.23) | copy-start | bytes 110596
  7.2 187.3 %all-gather.5.cloned.1.call-start = ((), (), s32[]{:S(2)}) async-start(), calls=%async_computation.7 | async-start | bytes 2506752 | tf_op jit(solution)/shard_map/all_gather | solution.py:97
  8.0 197.1 %all-gather.7.cloned.1.call-start = ((), (), s32[]{:S(2)}) async-start(), calls=%async_computation.8 | async-start | bytes 2506752 | tf_op jit(solution)/shard_map/all_gather | solution.py:100
  8.7 255.6 %all-gather.9.cloned.1.call-start = ((), (), s32[]{:S(2)}) async-start(), calls=%async_computation.9 | async-start | bytes 5013504 | tf_op jit(solution)/shard_map/all_gather | solution.py:154
  112.3 53.1 %copy-start.21 = (f32[128,256]{1,0:T(8,128)}, f32[128,256]{1,0:T(8,128)S(1)}, u32[]{:S(2)}) copy-start(f32[128,256]{1,0:T(8,128)S(1)} %get-tuple-element.73) | copy-start | bytes 393220
  112.5 86.5 %copy-start.40 = (f32[128]{0:T(128)}, f32[128]{0:T(128)S(1)}, u32[]{:S(2)}) copy-start(f32[128]{0:T(128)S(1)} %convert_bitcast_fusion.1) | copy-start | bytes 1540
  112.8 89.0 %copy-start.32 = (f32[128,128]{1,0:T(8,128)}, f32[128,128]{1,0:T(8,128)S(1)}, u32[]{:S(2)}) copy-start(f32[128,128]{1,0:T(8,128)S(1)} %get-tuple-element.66) | copy-start | bytes 196612
  112.9 89.0 %copy-start.34 = (f32[128,128]{1,0:T(8,128)}, f32[128,128]{1,0:T(8,128)S(1)}, u32[]{:S(2)}) copy-start(f32[128,128]{1,0:T(8,128)S(1)} %get-tuple-element.67) | copy-start | bytes 196612
  142.3 60.2 %copy-start.12 = (bf16[1024,256]{1,0:T(8,128)(2,1)}, bf16[1024,256]{1,0:T(8,128)(2,1)S(1)}, u32[]{:S(2)}) copy-start(bf16[1024,256]{1,0:T(8,128)(2,1)S(1)} %all_gather.47) | copy-start | bytes 1572868
  194.6 8.9 copy-start.36
  204.4 3.4 copy-start.42
  205.0 2.8 copy-start.19
  209.0 152.7 %reduce-scatter.8.cloned.1.call-start = ((), (), s32[]{:S(2)}) async-start(), calls=%async_computation.10 | async-start | bytes 5013504 | tf_op jit(solution)/shard_map/reduce_scatter | solution.py:159
  264.3 5.3 copy-start.44
  264.3 5.3 copy-start.46
  269.6 4.6 copy-start.52
  280.1 82.7 %copy-start.14 = (bf16[1,128,1152]{2,1,0:T(8,128)(2,1)S(1)}, bf16[1,128,1152]{2,1,0:T(8,128)(2,1)}, u32[]{:S(2)}) copy-start(bf16[1,128,1152]{2,1,0:T(8,128)(2,1)} %param.18) | copy-start | bytes 884740
  280.1 142.7 %all-gather.11.cloned.1.call-start = ((), (), s32[]{:S(2)}) async-start(), calls=%async_computation.11 | async-start | bytes 5013504 | tf_op jit(solution)/shard_map/all_gather | solution.py:170
  366.0 154.7 %reduce-scatter.10.cloned.1.call-start = ((), (), s32[]{:S(2)}) async-start(), calls=%async_computation.12 | async-start | bytes 5013504 | tf_op jit(solution)/shard_map/reduce_scatter | solution.py:177
  422.8 8.6 copy-start.45
  431.4 3.0 copy-start.49
  431.4 3.0 copy-start.50
  431.4 3.0 copy-start.47
  439.1 82.9 %copy-start.11 = (bf16[128,1152]{1,0:T(8,128)(2,1)S(1)}, bf16[128,1152]{1,0:T(8,128)(2,1)}, u32[]{:S(2)}) copy-start(bf16[128,1152]{1,0:T(8,128)(2,1)} %reduce-scatter.8.cloned.1.call-done) | copy-start | bytes 884740
  439.1 133.2 %reduce-scatter.12.cloned.1.call-start = ((), (), s32[]{:S(2)}) async-start(), calls=%async_computation.13 | async-start | bytes 1179648 | tf_op jit(solution)/shard_map/reduce_scatter | solution.py:205
  524.3 3.2 copy-start.9
  524.3 4.4 copy-start.43
  524.5 4.2 copy-start.6
  532.4 42.9 %copy-start.41 = (f32[128]{0:T(128)S(1)}, f32[128]{0:T(128)}, u32[]{:S(2)}) copy-start(f32[128]{0:T(128)} %copy-done.40) | copy-start | bytes 1540
  532.4 43.2 %copy-start.22 = (f32[128,256]{1,0:T(8,128)S(1)}, f32[128,256]{1,0:T(8,128)}, u32[]{:S(2)}) copy-start(f32[128,256]{1,0:T(8,128)} %copy-done.21) | copy-start | bytes 393220
  533.5 43.8 %copy-start.20 = (bf16[256,4,128]{2,0,1:T(8,128)(2,1)S(1)}, bf16[256,4,128]{2,0,1:T(8,128)(2,1)}, u32[]{:S(2)}) copy-start(bf16[256,4,128]{2,0,1:T(8,128)(2,1)} %copy-done.19) | copy-start | bytes 786436
  533.6 127.0 %reduce-scatter.18.cloned.1.call-start = ((), (), s32[]{:S(2)}) async-start(), calls=%async_computation.16 | async-start | bytes 626688 | tf_op jit(solution)/shard_map/reduce_scatter | solution.py:233
  574.4 131.6 %reduce-scatter.16.cloned.1.call-start = ((), (), s32[]{:S(2)}) async-start(), calls=%async_computation.15 | async-start | bytes 626688 | tf_op jit(solution)/shard_map/reduce_scatter | solution.py:230
  577.3 203.8 %reduce-scatter.20.cloned.1.call-start = ((), (), s32[]{:S(2)}) async-start(), calls=%async_computation.17 | async-start | bytes 2506752 | tf_op jit(solution)/shard_map/reduce_scatter | solution.py:236
  579.6 276.8 %reduce-scatter.14.cloned.1.call-start = ((), (), s32[]{:S(2)}) async-start(), calls=%async_computation.14 | async-start | bytes 2506752 | tf_op jit(solution)/shard_map/reduce_scatter | solution.py:227
  583.7 7.9 slice-start
  583.7 344.6 %all-reduce.19.cloned.1.call-start = ((), (), s32[]{:S(2)}) async-start(), calls=%async_computation.18 | async-start | bytes 153600 | tf_op jit(solution)/shard_map/psum | solution.py:260
  585.1 6.5 slice-start.1
  585.1 6.5 copy-start.51
  591.7 3.4 copy-start.3
  706.0 378.8 %all-reduce.21.cloned.1.call-start = ((), (), s32[]{:S(2)}) async-start(), calls=%async_computation.19 | async-start | bytes 6561792 | tf_op jit(solution)/shard_map/psum | solution.py:259
  712.3 144.1 %copy-start.10 = (f32[128,1152]{1,0:T(8,128)S(1)}, f32[128,1152]{1,0:T(8,128)}, u32[]{:S(2)}) copy-start(f32[128,1152]{1,0:T(8,128)} %copy-done.9) | copy-start | bytes 1769476
  1084.7 6.1 copy-start.31
  1088.1 4.1 copy-start.30
  1090.8 2.8 copy-start.1
  (21 other events, 33.9 us)
Sparse Core Ops, SparseCore 0:
  10.5 51.5 all-gather.4
  64.5 49.3 all-gather.6
  209.1 55.2 all-gather.8
  280.3 81.4 reduce-scatter.7
  366.2 56.6 all-gather.10
  439.2 81.4 reduce-scatter.9
  533.7 38.5 reduce-scatter.11
  576.0 62.8 reduce-scatter.17
  642.6 63.2 reduce-scatter.15
  709.8 71.2 reduce-scatter.19
  785.0 71.2 reduce-scatter.13
  859.8 68.4 all-reduce.18
  932.1 152.6 all-reduce.20
where the time goes:
time: 1100 us
  waiting for transfers between devices  722 us (66%)
  blocking collectives  232 us (21%)
  matrix products  69.1 us (6%)
  other arithmetic  35.6 us (3%)
  local copies, waits for them, and re-layouts  22.2 us (2%)
  between operations  17.4 us (2%)
    psum x1, waiting for transfers between devices, body(): lax.psum(shards[0].astype(jnp.bfloat16), 'ctx').astype(jnp.float32)  147 us
    unnamed x2, blocking collectives  125 us
    reduce_scatter x1, waiting for transfers between devices, body(): lax.psum_scatter((jnp.dot(grad_gate, w_gate, preferred_element_type=f32)...  81.6 us
    reduce_scatter x1, waiting for transfers between devices, body(): lax.psum_scatter(jnp.dot(hidden, w_down, preferred_element_type=f32).asty...  81.5 us
    reduce_scatter x1, waiting for transfers between devices, body(): lax.psum_scatter(term_query.astype(jnp.bfloat16), 'fsdp', scatter_dimensi...  75.3 us
    psum x1, waiting for transfers between devices, body(): lax.psum(shards[1].astype(jnp.bfloat16), 'ctx').astype(jnp.float32)  71 us
    reduce_scatter x1, waiting for transfers between devices, body(): lax.psum_scatter(term_output.astype(jnp.bfloat16), 'fsdp', scatter_dimens...  68.7 us
    all_gather x1, waiting for transfers between devices, body(): grad_all = lax.all_gather(grad_ffn, 'fsdp', axis=0, tiled=True)  56.5 us
  transfers between devices with their start and end apart: 13, of which 10 were waited for; matrix products, arithmetic and copies ran while one was open for 5% of the time, Pallas kernels for 0%

commit v1 on v0

--- a/solution.py
+++ b/solution.py
@@ -93,9 +93,22 @@
     parts = lax.axis_size("ctx")
     total = local * parts
     block = local // 2
+
+    def scan_limits(m, join_dim=0):
+        z1 = jnp.concatenate(
+            jax.lax.all_to_all(
+                jnp.stack(jax.lax.axis_size("fsdp") * [m]),
+                axis_name="fsdp",
+                split_axis=0,
+                concat_axis=0,
+            ),
+            axis=join_dim,
+        )
+        return z1
+
     gathered = (
         lax.all_gather(w_query, "fsdp", axis=0, tiled=True),
-        lax.all_gather(w_key, "fsdp", axis=0, tiled=True),
+        scan_limits(w_key),
         lax.all_gather(w_value, "fsdp", axis=0, tiled=True),
         lax.all_gather(w_output, "fsdp", axis=1, tiled=True),
         lax.all_gather(gain_in, "fsdp", axis=0, tiled=True),

time: 1100 us -> 1080 us (0.982)
  blocking collectives: 232 us -> 209 us
    all_gather x1 -> x0, blocking collectives: 26.9 us -> none  [body(): lax.all_gather(w_key, 'fsdp', axis=0, tiled=True)]
  transfers between devices with their start and end apart: 13 -> 14, of which waited for: 10 -> 10; matrix products, arithmetic and copies ran while one was open for 5% -> 5% of each run, Pallas kernels for 0% -> 0%
where the time goes in v1:
time: 1080 us
  waiting for transfers between devices  723 us (67%)
  blocking collectives  209 us (19%)
  matrix products  67.9 us (6%)
  other arithmetic  36.5 us (3%)
  local copies, waits for them, and re-layouts  19.3 us (2%)
  between operations  17.5 us (2%)
    psum x1, waiting for transfers between devices, body(): lax.psum(shards[0].astype(jnp.bfloat16), 'ctx').astype(jnp.float32)  147 us
    unnamed x2, blocking collectives  124 us
    reduce_scatter x1, waiting for transfers between devices, body(): lax.psum_scatter((jnp.dot(grad_gate, w_gate, preferred_element_type=f32)...  81.6 us
    reduce_scatter x1, waiting for transfers between devices, body(): lax.psum_scatter(jnp.dot(hidden, w_down, preferred_element_type=f32).asty...  81.5 us
    reduce_scatter x1, waiting for transfers between devices, body(): lax.psum_scatter(term_query.astype(jnp.bfloat16), 'fsdp', scatter_dimensi...  75.3 us
    psum x1, waiting for transfers between devices, body(): lax.psum(shards[1].astype(jnp.bfloat16), 'ctx').astype(jnp.float32)  71.1 us
    reduce_scatter x1, waiting for transfers between devices, body(): lax.psum_scatter(term_output.astype(jnp.bfloat16), 'fsdp', scatter_dimens...  68.7 us
    all_gather x1, waiting for transfers between devices, body(): grad_all = lax.all_gather(grad_ffn, 'fsdp', axis=0, tiled=True)  56.5 us
  transfers between devices with their start and end apart: 14, of which 10 were waited for; matrix products, arithmetic and copies ran while one was open for 5% of the time, Pallas kernels for 0%

profile of v1, /device:TPU:8, one launch (start us, length us, event | category | flops | bytes accessed | tf_op | source)
XLA Modules:
  0.0 1082.4 jit_solution(5077661041885405316)
XLA Ops:
  8.0 1.6 stack.2
  9.6 8.2 all-to-all-start
  18.7 1.3 fusion.102
  24.9 64.5 %all-reduce.13 = (bf16[1152]{0:T(1024)(128)(2,1)S(1)}, bf16[256]{0:T(256)(128)(2,1)S(1)}, bf16[256]{0:T(256)(128)(2,1)S(1)}, bf16[1152]{0:T(1024)(128)(2,1)S(1)}...) all-reduce(bf16[1152]{0:T(1024)(128)(2,1)S(1)} %dynamic-update-slic, ...), channel_id=1, replica_groups=mesh['ctx'=8,'fsdp'=16] {'fsdp'}, use_global_device_ids=true, to_apply=%add | all-reduce | flops 5120 | bytes 20480
  89.8 26.5 %all_gather.40 = bf16[1152,256]{1,0:T(8,128)(2,1)S(1)} all-gather(bf16[72,256]{1,0:T(8,128)(2,1)S(1)} %copy-done.39), channel_id=1, replica_groups=mesh['ctx'=8,'fsdp'=16] {'fsdp'}, dimensions={0}, use_global_device_ids=true | all-gather | bytes 626688 | tf_op jit(solution)/shard_map/all_gather | solution.py:112
  117.1 29.3 %all_gather.41 = bf16[1024,256]{1,0:T(8,128)(2,1)S(1)} all-gather(bf16[128,256]{1,0:T(8,128)(2,1)S(1)} %convolution_convert_fusion.10), channel_id=1, replica_groups=mesh['ctx'=8,'fsdp'=16] {'ctx'}, dimensions={0}, use_global_device_ids=true | all-gather | bytes 589824 | tf_op jit(solution)/shard_map/all_gather | solution.py:148
  147.3 28.9 %all_gather.43 = bf16[1024,256]{1,0:T(8,128)(2,1)S(1)} all-gather(bf16[128,256]{1,0:T(8,128)(2,1)S(1)} %pad_maximum_fusion.3), channel_id=1, replica_groups=mesh['ctx'=8,'fsdp'=16] {'ctx'}, dimensions={0}, use_global_device_ids=true | all-gather | bytes 589824 | tf_op jit(solution)/shard_map/all_gather | solution.py:147
  176.2 4.5 copy.77
  180.7 2.6 multiply_reduce_fusion.7
  186.8 2.7 multiply_reduce_fusion.3
  190.9 55.7 %all-gather.9.cloned.1.call-done = bf16[2048,1152]{1,0:T(8,128)(2,1)} async-done(((bf16[128,1152]{1,0:T(8,128)(2,1)}), bf16[2048,1152]{1,0:T(8,128)(2,1)}) %all-gather.9.cloned.1.call-update) | async-done | bytes 4718608 | tf_op jit(solution)/shard_map/all_gather | solution.py:167
  246.6 5.3 fusion.103
  251.9 4.6 multiply_convert_fusion.1
  257.7 4.7 convolution_convert_fusion
  262.5 81.5 %reduce-scatter.8.cloned.1.call-done = bf16[128,1152]{1,0:T(8,128)(2,1)} async-done(((bf16[2048,1152]{1,0:T(8,128)(2,1)}), bf16[128,1152]{1,0:T(8,128)(2,1)}) %reduce-scatter.8.cloned.1.call-update) | async-done | bytes 294928 | tf_op jit(solution)/shard_map/reduce_scatter | solution.py:172
  345.1 1.3 fusion.46
  346.4 1.9 fusion.28
  348.6 56.5 %all-gather.11.cloned.1.call-done = bf16[2048,1152]{1,0:T(8,128)(2,1)} async-done(((bf16[128,1152]{1,0:T(8,128)(2,1)}), bf16[2048,1152]{1,0:T(8,128)(2,1)}) %all-gather.11.cloned.1.call-update) | async-done | bytes 4718608 | tf_op jit(solution)/shard_map/all_gather | solution.py:183
  405.1 8.5 multiply_convert_fusion
  413.7 3.0 fusion.104
  416.7 4.6 add_convert_fusion
  421.4 81.6 %reduce-scatter.10.cloned.1.call-done = bf16[128,1152]{1,0:T(8,128)(2,1)} async-done(((bf16[2048,1152]{1,0:T(8,128)(2,1)}), bf16[128,1152]{1,0:T(8,128)(2,1)}) %reduce-scatter.10.cloned.1.call-update) | async-done | bytes 294928 | tf_op jit(solution)/shard_map/reduce_scatter | solution.py:190
  502.9 1.3 fusion.35
  504.2 2.3 multiply_reduce_fusion
  506.7 1.2 convolution_convert_fusion.8
  508.0 1.8 copy.80
  511.0 1.5 fusion.12
  515.8 38.5 %reduce-scatter.12.cloned.1.call-done = bf16[128,512]{1,0:T(8,128)(2,1)} async-done(((bf16[1024,512]{1,0:T(8,128)(2,1)}), bf16[128,512]{1,0:T(8,128)(2,1)}) %reduce-scatter.12.cloned.1.call-update) | async-done | bytes 131088 | tf_op jit(solution)/shard_map/reduce_scatter | solution.py:218
  554.4 2.1 convolution_convert_fusion.6
  558.1 1.3 convolution_convert_fusion.7
  559.5 2.2 convolution_convert_fusion.1
  563.5 2.3 convolution_convert_fusion.2
  567.3 6.5 convolution_convert_fusion.3
  573.8 3.4 convolution_convert_fusion.4
  579.1 59.8 %all-reduce.12 = (bf16[1152]{0:T(1024)(128)(2,1)S(1)}, bf16[256]{0:T(256)(128)(2,1)S(1)}, bf16[256]{0:T(256)(128)(2,1)S(1)}, bf16[1152]{0:T(1024)(128)(2,1)S(1)}...) all-reduce(bf16[1152]{0:T(1024)(128)(2,1)S(1)} %get-tuple-element.2, ...), channel_id=9, replica_groups=mesh['ctx'=8,'fsdp'=16] {'fsdp'}, use_global_device_ids=true, to_apply=%region_32.33.clone | all-reduce | flops 5120 | bytes 20480
  642.4 45.7 %reduce-scatter.16.cloned.1.call-done = bf16[72,256]{1,0:T(8,128)(2,1)} async-done(((bf16[1152,256]{1,0:T(8,128)(2,1)}), bf16[72,256]{1,0:T(8,128)(2,1)}) %reduce-scatter.16.cloned.1.call-update) | async-done | bytes 36880 | tf_op jit(solution)/shard_map/reduce_scatter | solution.py:243
  688.2 6.3 convolution_convert_fusion.5
  694.5 68.7 %reduce-scatter.20.cloned.1.call-done = bf16[1024,72]{0,1:T(8,128)(2,1)} async-done(((bf16[1024,1152]{0,1:T(8,128)(2,1)}), bf16[1024,72]{0,1:T(8,128)(2,1)}) %reduce-scatter.20.cloned.1.call-update) | async-done | bytes 147472 | tf_op jit(solution)/shard_map/reduce_scatter | solution.py:249
  763.2 75.3 %reduce-scatter.14.cloned.1.call-done = bf16[72,1024]{1,0:T(8,128)(2,1)} async-done(((bf16[1152,1024]{1,0:T(8,128)(2,1)}), bf16[72,1024]{1,0:T(8,128)(2,1)}) %reduce-scatter.14.cloned.1.call-update) | async-done | bytes 147472 | tf_op jit(solution)/shard_map/reduce_scatter | solution.py:240
  839.5 71.1 %all-reduce.19.cloned.1.call-done = (bf16[72,256]{1,0:T(8,128)(2,1)}, bf16[72,256]{1,0:T(8,128)(2,1)}, bf16[72]{0:T(256)(128)(2,1)}, bf16[16]{0:T(256)(128)(2,1)...) async-done(((bf16[72,256]{1,0:T(8,128)(2,1)}, bf16[72,256]{1,0:T(8,128)(2,1)}, bf16[72]{0:T(256)(128)(2,1)}, ...) | async-done | bytes 74384 | tf_op jit(solution)/shard_map/psum | solution.py:273
  917.6 1.4 convert_element_type.283
  919.0 1.4 convert_element_type.285
  920.4 146.6 %all-reduce.21.cloned.1.call-done = (bf16[72,1024]{1,0:T(8,128)(2,1)}, bf16[1024,72]{0,1:T(8,128)(2,1)}, bf16[432,1152]{1,0:T(8,128)(2,1)}, bf16[432,1152]{1,0:T(8,128)(2,1)}, bf16[432,1152]{1,0:T(8,128)(2,1)}) async-done(((bf16[72,1024]{1,0:T(8,128)(2,1)}, bf16[1024,72]{0,1:T(8,128)(2,1)}, bf16[432,1152]{1,0:T(8,128)(2,1)}, bf16[432,1152]{1,0:T(8,128)(2,1)}, bf16[432,1152]{1,0:T(8,128)(2,1)}), ...) | async-done | bytes 3280912 | tf_op jit(solution)/shard_map/psum | solution.py:272
  1067.0 1.7 convert_element_type.281
  1068.7 1.6 convert_element_type.287
  1070.4 2.7 convert_element_type.289
  1073.1 1.4 convert_element_type.291
  1074.5 1.4 convert_element_type.293
  (241 shorter events, 36.0 us)
Async XLA Ops:
  7.2 250.5 %copy-start = (bf16[432,1152]{1,0:T(8,128)(2,1)S(1)}, bf16[432,1152]{1,0:T(8,128)(2,1)}, u32[]{:S(2)}) copy-start(bf16[432,1152]{1,0:T(8,128)(2,1)} %param.27) | copy-start | bytes 2985988
  7.2 109.1 %copy-start.2 = (bf16[1,128,1152]{2,1,0:T(8,128)(2,1)S(1)}, bf16[1,128,1152]{2,1,0:T(8,128)(2,1)}, u32[]{:S(2)}) copy-start(bf16[1,128,1152]{2,1,0:T(8,128)(2,1)} %param.17) | copy-start | bytes 884740
  7.2 15.9 %copy-start.44 = (s32[8,2]{0,1:T(2,128)S(1)}, s32[8,2]{0,1:T(2,128)}, u32[]{:S(2)}) copy-start(s32[8,2]{0,1:T(2,128)} %param.20) | copy-start | bytes 196
  7.2 16.2 %copy-start.49 = (bf16[16]{0:T(256)(128)(2,1)S(1)}, bf16[16]{0:T(256)(128)(2,1)}, u32[]{:S(2)}) copy-start(bf16[16]{0:T(256)(128)(2,1)} %param.30) | copy-start | bytes 100
  7.2 16.4 %copy-start.50 = (bf16[16]{0:T(256)(128)(2,1)S(1)}, bf16[16]{0:T(256)(128)(2,1)}, u32[]{:S(2)}) copy-start(bf16[16]{0:T(256)(128)(2,1)} %param.29) | copy-start | bytes 100
  7.2 16.7 %copy-start.51 = (bf16[72]{0:T(256)(128)(2,1)S(1)}, bf16[72]{0:T(256)(128)(2,1)}, u32[]{:S(2)}) copy-start(bf16[72]{0:T(256)(128)(2,1)} %param.32) | copy-start | bytes 436
  7.3 16.9 %copy-start.52 = (bf16[72]{0:T(256)(128)(2,1)S(1)}, bf16[72]{0:T(256)(128)(2,1)}, u32[]{:S(2)}) copy-start(bf16[72]{0:T(256)(128)(2,1)} %param.31) | copy-start | bytes 436
  7.3 17.2 %copy-start.53 = (bf16[72]{0:T(256)(128)(2,1)S(1)}, bf16[72]{0:T(256)(128)(2,1)}, u32[]{:S(2)}) copy-start(bf16[72]{0:T(256)(128)(2,1)} %param.28) | copy-start | bytes 436
  7.3 17.4 %copy-start.54 = (bf16[72]{0:T(256)(128)(2,1)S(1)}, bf16[72]{0:T(256)(128)(2,1)}, u32[]{:S(2)}) copy-start(bf16[72]{0:T(256)(128)(2,1)} %param.33) | copy-start | bytes 436
  7.3 82.5 %copy-start.39 = (bf16[72,256]{1,0:T(8,128)(2,1)S(1)}, bf16[72,256]{1,0:T(8,128)(2,1)}, u32[]{:S(2)}) copy-start(bf16[72,256]{1,0:T(8,128)(2,1)} %param.23) | copy-start | bytes 110596
  7.3 168.9 %all-gather.5.cloned.1.call-start = ((), (), s32[]{:S(2)}) async-start(), calls=%async_computation.8 | async-start | bytes 2506752 | tf_op jit(solution)/shard_map/all_gather | solution.py:110
  9.6 136.7 %all-to-all-start = ((bf16[16,72,256]{2,1,0:T(8,128)(2,1)}), bf16[16,72,256]{2,1,0:T(8,128)(2,1)S(1)}, u32[]{:S(2)}, u32[]{:S(2)}) async-start(bf16[16,72,256]{2,1,0:T(8,128)(2,1)} %stack.2), calls=%async_computation | async-start | bytes 1179648 | tf_op jit(solution)/shard_map/all_to_all | solution.py:99
  17.9 168.9 %all-gather.7.cloned.1.call-start = ((), (), s32[]{:S(2)}) async-start(), calls=%async_computation.9 | async-start | bytes 2506752 | tf_op jit(solution)/shard_map/all_gather | solution.py:113
  18.6 227.9 %all-gather.9.cloned.1.call-start = ((), (), s32[]{:S(2)}) async-start(), calls=%async_computation.10 | async-start | bytes 5013504 | tf_op jit(solution)/shard_map/all_gather | solution.py:167
  116.3 64.4 %copy-start.40 = (f32[128]{0:T(128)}, f32[128]{0:T(128)S(1)}, u32[]{:S(2)}) copy-start(f32[128]{0:T(128)S(1)} %multiply_power_fusion) | copy-start | bytes 1540
  146.4 38.8 %copy-start.36 = (bf16[1024,256]{1,0:T(8,128)(2,1)}, bf16[1024,256]{1,0:T(8,128)(2,1)S(1)}, u32[]{:S(2)}) copy-start(bf16[1024,256]{1,0:T(8,128)(2,1)S(1)} %all_gather.41) | copy-start | bytes 1572868
  146.8 34.0 %copy-start.21 = (f32[128,256]{1,0:T(8,128)}, f32[128,256]{1,0:T(8,128)S(1)}, u32[]{:S(2)}) copy-start(f32[128,256]{1,0:T(8,128)S(1)} %get-tuple-element.73) | copy-start | bytes 393220
  147.2 36.3 %copy-start.32 = (f32[128,128]{1,0:T(8,128)}, f32[128,128]{1,0:T(8,128)S(1)}, u32[]{:S(2)}) copy-start(f32[128,128]{1,0:T(8,128)S(1)} %get-tuple-element.66) | copy-start | bytes 196612
  147.2 36.3 %copy-start.34 = (f32[128,128]{1,0:T(8,128)}, f32[128,128]{1,0:T(8,128)S(1)}, u32[]{:S(2)}) copy-start(f32[128,128]{1,0:T(8,128)S(1)} %get-tuple-element.67) | copy-start | bytes 196612
  176.2 8.0 copy-start.12
  190.7 153.3 %reduce-scatter.8.cloned.1.call-start = ((), (), s32[]{:S(2)}) async-start(), calls=%async_computation.11 | async-start | bytes 5013504 | tf_op jit(solution)/shard_map/reduce_scatter | solution.py:172
  246.6 5.3 copy-start.45
  246.6 5.3 copy-start.47
  251.9 4.6 copy-start.58
  262.4 82.7 %copy-start.14 = (bf16[1,128,1152]{2,1,0:T(8,128)(2,1)S(1)}, bf16[1,128,1152]{2,1,0:T(8,128)(2,1)}, u32[]{:S(2)}) copy-start(bf16[1,128,1152]{2,1,0:T(8,128)(2,1)} %param.18) | copy-start | bytes 884740
  262.4 142.7 %all-gather.11.cloned.1.call-start = ((), (), s32[]{:S(2)}) async-start(), calls=%async_computation.12 | async-start | bytes 5013504 | tf_op jit(solution)/shard_map/all_gather | solution.py:183
  348.3 154.6 %reduce-scatter.10.cloned.1.call-start = ((), (), s32[]{:S(2)}) async-start(), calls=%async_computation.13 | async-start | bytes 5013504 | tf_op jit(solution)/shard_map/reduce_scatter | solution.py:190
  405.1 8.6 copy-start.46
  421.3 82.9 %copy-start.11 = (bf16[128,1152]{1,0:T(8,128)(2,1)S(1)}, bf16[128,1152]{1,0:T(8,128)(2,1)}, u32[]{:S(2)}) copy-start(bf16[128,1152]{1,0:T(8,128)(2,1)} %reduce-scatter.8.cloned.1.call-done) | copy-start | bytes 884740
  421.3 133.0 %reduce-scatter.12.cloned.1.call-start = ((), (), s32[]{:S(2)}) async-start(), calls=%async_computation.14 | async-start | bytes 1179648 | tf_op jit(solution)/shard_map/reduce_scatter | solution.py:218
  506.5 4.4 copy-start.43
  506.7 4.2 copy-start.6
  514.6 42.8 %copy-start.41 = (f32[128]{0:T(128)S(1)}, f32[128]{0:T(128)}, u32[]{:S(2)}) copy-start(f32[128]{0:T(128)} %copy-done.40) | copy-start | bytes 1540
  514.7 43.1 %copy-start.22 = (f32[128,256]{1,0:T(8,128)S(1)}, f32[128,256]{1,0:T(8,128)}, u32[]{:S(2)}) copy-start(f32[128,256]{1,0:T(8,128)} %copy-done.21) | copy-start | bytes 393220
  515.8 43.7 %copy-start.20 = (bf16[256,4,128]{2,0,1:T(8,128)(2,1)S(1)}, bf16[256,4,128]{2,0,1:T(8,128)(2,1)}, u32[]{:S(2)}) copy-start(bf16[256,4,128]{2,0,1:T(8,128)(2,1)} %copy-done.19) | copy-start | bytes 786436
  515.8 126.7 %reduce-scatter.18.cloned.1.call-start = ((), (), s32[]{:S(2)}) async-start(), calls=%async_computation.17 | async-start | bytes 626688 | tf_op jit(solution)/shard_map/reduce_scatter | solution.py:246
  556.5 131.6 %reduce-scatter.16.cloned.1.call-start = ((), (), s32[]{:S(2)}) async-start(), calls=%async_computation.16 | async-start | bytes 626688 | tf_op jit(solution)/shard_map/reduce_scatter | solution.py:243
  559.4 203.8 %reduce-scatter.20.cloned.1.call-start = ((), (), s32[]{:S(2)}) async-start(), calls=%async_computation.18 | async-start | bytes 2506752 | tf_op jit(solution)/shard_map/reduce_scatter | solution.py:249
  561.7 276.7 %reduce-scatter.14.cloned.1.call-start = ((), (), s32[]{:S(2)}) async-start(), calls=%async_computation.15 | async-start | bytes 2506752 | tf_op jit(solution)/shard_map/reduce_scatter | solution.py:240
  565.9 7.9 slice-start
  565.9 344.7 %all-reduce.19.cloned.1.call-start = ((), (), s32[]{:S(2)}) async-start(), calls=%async_computation.19 | async-start | bytes 153600 | tf_op jit(solution)/shard_map/psum | solution.py:273
  567.3 6.5 slice-start.1
  567.3 6.5 copy-start.57
  573.8 3.4 copy-start.3
  688.1 378.8 %all-reduce.21.cloned.1.call-start = ((), (), s32[]{:S(2)}) async-start(), calls=%async_computation.20 | async-start | bytes 6561792 | tf_op jit(solution)/shard_map/psum | solution.py:272
  694.5 144.1 %copy-start.10 = (f32[128,1152]{1,0:T(8,128)S(1)}, f32[128,1152]{1,0:T(8,128)}, u32[]{:S(2)}) copy-start(f32[128,1152]{1,0:T(8,128)} %copy-done.9) | copy-start | bytes 1769476
  1067.0 6.1 copy-start.31
  1070.4 4.1 copy-start.30
  (28 other events, 54.0 us)
Sparse Core Ops, SparseCore 0:
  10.6 52.4 all-gather.4
  65.5 48.7 all-gather.6
  190.8 55.7 all-gather.8
  262.5 81.4 reduce-scatter.7
  348.4 56.6 all-gather.10
  421.5 81.4 reduce-scatter.9
  515.9 38.4 reduce-scatter.11
  558.1 62.8 reduce-scatter.17
  624.8 63.3 reduce-scatter.15
  691.9 71.2 reduce-scatter.19
  767.2 71.2 reduce-scatter.13
  842.0 68.5 all-reduce.18
  914.3 152.6 all-reduce.20
